TPU v7x, 128 devices: a whole 4x4x4 slice. The times are simulated.
128 devices in a mesh: child: 2 (over z_lo), row: 16 (over x, y), col: 4 (over z_hi, core).
Axes of the slice: x: 4, y: 4, z: 4 (z_hi: 2, z_lo: 2; z = z_hi * 2 + z_lo), core: 2. Of those that a mesh axis runs over, the one named last changes fastest.
Arguments:
- child_fronts: float32 [2, 4096, 4096], P('child', 'row', 'col'), as said below
- root_front: float32 [8192, 8192], P('col', ('child', 'row')), as said below
- block_maps: int32 [2, 24], replicated, may hold values from 0 to 63, as said below
Outputs:
- child_factor: float32 [2, 4096, 1024], P('child', 'row')
- root_factor: float32 [8192, 512], P('col')
- root_trailing: float32 [8192, 8192], P('col', ('child', 'row'))
Inputs may be any that keep to these rules, and one draw needn't show every extreme that they name: `block_maps`: row c lists 24 different root blocks in increasing order; block 0 appears in the first row and the last root block in the last row. `child_fronts`: each front is symmetric and positive definite. `root_front`: symmetric and positive definite.
All inputs are finite; a program needn't handle non-finite values.
Results may differ from a plain program's by a relative error of at most 0.0003.
Values may be sent and summed in bfloat16 or wider, within the bound.
No kernel may reach another device: no remote copies, remote signals or barrier semaphores. Data moves between devices by JAX's collectives and lax.ppermute only.
A program may use at most 128 MiB of HBM per device.

v0:
```python
import jax
import jax.numpy as jnp
from jax import lax
from jax.sharding import PartitionSpec as P

R = 8192
PANEL = 512
CPAN = 2
BLK = 128
PIV = 1024
NCB = 24


def from_root(block, axis, holder):
    block = jnp.where(lax.axis_index(axis) == holder, block, jnp.zeros_like(block))
    return lax.psum(block, axis)


def lookup(table, first_idx, second_idx):
    hits = (first_idx[..., None, None] == jnp.arange(table.shape[0], dtype=jnp.int32)[:, None]) & (
        second_idx[..., None, None] == jnp.arange(table.shape[1], dtype=jnp.int32)[None, :]
    )
    return jnp.sum(jnp.where(hits, table, 0), axis=(-2, -1))


def panel_step(local_tile, first_col, is_root):
    row_block, col_block = local_tile.shape
    if is_root:
        row_pos = lax.axis_index("col")
        col_pos = lax.axis_index(("child", "row"))
    else:
        row_pos = lax.axis_index("row")
        col_pos = lax.axis_index("col")
    panel_width = min(PANEL, col_block)
    offset = first_col % col_block if col_block >= PANEL else 0
    portion = lax.slice_in_dim(local_tile, offset, offset + panel_width, axis=1)
    arrived = []
    for member in range(max(PANEL // col_block, 1)):
        holder = first_col // col_block + member
        if is_root:
            arrived.append(from_root(portion, ("child", "row"), holder))
        else:
            arrived.append(from_root(portion, "col", holder))
    panel_rows = jnp.concatenate(arrived, axis=1)
    diag_width = min(PANEL, row_block)
    diag_offset = first_col % row_block if row_block >= PANEL else 0
    diag_portion = lax.slice_in_dim(panel_rows, diag_offset, diag_offset + diag_width, axis=0)
    diag_parts = []
    for member in range(max(PANEL // row_block, 1)):
        holder = first_col // row_block + member
        if is_root:
            diag_parts.append(from_root(diag_portion, "col", holder))
        else:
            diag_parts.append(from_root(diag_portion, "row", holder))
    diagonal = jnp.concatenate(diag_parts, axis=0)
    diag_factor = jnp.linalg.cholesky(diagonal)
    solved = lax.linalg.triangular_solve(
        diag_factor, panel_rows, left_side=False, lower=True, transpose_a=True
    )
    row_ids = row_pos * row_block + jnp.arange(row_block, dtype=jnp.int32)
    factor_rows = jnp.where(row_ids[:, None] >= first_col, solved, 0.0)
    update_rows = jnp.where(row_ids[:, None] >= first_col + PANEL, solved, 0.0).astype(jnp.bfloat16)
    if is_root:
        all_rows = lax.all_gather(update_rows, "col", axis=0, tiled=True)
    else:
        all_rows = lax.all_gather(update_rows, "row", axis=0, tiled=True)
    column_rows = lax.dynamic_slice_in_dim(all_rows, col_pos * col_block, col_block, 0)
    update = lax.dot_general(
        update_rows, column_rows, (((1,), (1,)), ((), ())), preferred_element_type=jnp.float32
    )
    return (local_tile - update, factor_rows)


def local(child_fronts, root_front, block_maps):
    local_tile = child_fronts[0]
    factors = []
    for panel_index in range(CPAN):
        local_tile, factor_rows = panel_step(local_tile, panel_index * PANEL, False)
        factors.append(factor_rows)
    child_factor = jnp.concatenate(factors, axis=1)[None]
    row_block, col_block = local_tile.shape
    child_pos = lax.axis_index("child")
    col_pos = lax.axis_index("col")
    row_count = lax.axis_size("row")
    group_count = lax.axis_size(("child", "row"))
    col_count = lax.axis_size("col")
    row_blocks = row_block // BLK
    root_blocks = R // BLK
    target_blocks = R // col_count // BLK
    width_out = R // group_count
    sources = jnp.arange(group_count, dtype=jnp.int32)
    front_blocks = (sources % row_count)[:, None] * row_blocks + jnp.arange(
        row_blocks, dtype=jnp.int32
    )[None, :]
    contrib_rows = front_blocks - PIV // BLK
    source_child = jnp.broadcast_to((sources // row_count)[:, None], contrib_rows.shape)
    row_targets = lookup(block_maps, source_child, contrib_rows)
    row_valid = contrib_rows >= 0
    block_ids = jnp.arange(root_blocks, dtype=jnp.int32)
    full_rows = lax.all_gather(local_tile, "col", axis=1, tiled=True)
    contrib = full_rows[:, PIV:].reshape(row_block, NCB, BLK)
    col_targets = lookup(
        block_maps, jnp.full((NCB,), child_pos, dtype=jnp.int32), jnp.arange(NCB, dtype=jnp.int32)
    )
    col_table = (col_targets[:, None] == block_ids[None, :]).astype(jnp.float32)
    placed = jnp.einsum("ray,am->rmy", contrib, col_table, precision=lax.Precision.HIGHEST).reshape(
        row_block, group_count, width_out
    )
    keep_rows = row_valid & (row_targets // target_blocks == col_pos)
    row_table = (
        keep_rows[:, :, None]
        & (
            (row_targets % target_blocks)[:, :, None]
            == jnp.arange(target_blocks, dtype=jnp.int32)[None, None, :]
        )
    ).astype(jnp.float32)
    received = lax.all_to_all(placed, ("child", "row"), split_axis=1, concat_axis=0, tiled=True)
    count_cols = received.shape[2]
    stacked = received.reshape(group_count, row_blocks, BLK, count_cols)
    summed = jnp.einsum("stq,stxn->qxn", row_table, stacked, precision=lax.Precision.HIGHEST)
    added = summed.reshape(target_blocks * BLK, count_cols)
    assembled = root_front + added
    panel_index = 0
    assembled, factor_rows = panel_step(assembled, panel_index * PANEL, True)
    return (child_factor, factor_rows, assembled)


def solution(mesh):
    return jax.shard_map(
        local,
        mesh=mesh,
        in_specs=(P("child", "row", "col"), P("col", ("child", "row")), P()),
        out_specs=(P("child", "row", None), P("col", None), P("col", ("child", "row"))),
        check_vma=False,
    )
```

profile of v0, /device:TPU:1, one launch (start us, length us, event | category | flops | bytes accessed | tf_op | source)
XLA Modules:
  0.0 1564.4 jit_solution(4274154260043947339)
XLA Ops:
  9.7 47.3 %all-reduce.11.cloned.1.call-done = f32[256,512]{0,1:T(8,128)} async-done(((f32[256,512]{0,1:T(8,128)}), f32[256,512]{0,1:T(8,128)}) %all-reduce.11.cloned.1.call-update) | async-done | bytes 524304 | tf_op jit(solution)/shard_map/psum | solution.py:16
  59.1 85.8 %all-reduce.21.cloned.1.call-done = (f32[256,512]{0,1:T(8,128)}, f32[256,512]{0,1:T(8,128)}) async-done(((f32[256,512]{0,1:T(8,128)}, f32[256,512]{0,1:T(8,128)}), (f32[256,512]{0,1:T(8,128)}, f32[256,512]{0,1:T(8,128)})) %all-reduce.21.cloned.1.call-update) | async-done | bytes 1048592 | tf_op jit(solution)/shard_map/psum | solution.py:16
  148.8 11.7 cholesky.374
  160.5 9.8 custom-call.34
  173.0 11.7 cholesky.393
  184.7 10.0 custom-call.35
  196.3 11.7 cholesky.414
  208.8 9.8 custom-call.36
  220.1 11.7 cholesky.431
  232.4 12.5 compare_reduce_fusion.10
  247.7 8.0 while.6
  255.7 39.3 %custom-call.37 = f32[4,128,128]{1,2,0:T(8,128)S(1)} custom-call(f32[4,128,128]{2,1,0:T(8,128)S(1)} %get-tuple-element.27), custom_call_target="InvertDiagBlocksLowerTriangular" | custom-call | tf_op jit(solution)/shard_map/triangular_solve/custom-call.3 | solution.py:57
  301.9 57.4 %all-gather.5.cloned.1.call-done = bf16[4096,512]{0,1:T(8,128)(2,1)} async-done(((bf16[256,512]{0,1:T(8,128)(2,1)}), bf16[4096,512]{0,1:T(8,128)(2,1)}) %all-gather.5.cloned.1.call-update) | async-done | bytes 4194320 | tf_op jit(solution)/shard_map/all_gather | solution.py:66
  362.0 43.1 %all-reduce.13.cloned.1.call-done = f32[256,512]{0,1:T(8,128)} async-done(((f32[256,512]{0,1:T(8,128)}), f32[256,512]{0,1:T(8,128)}) %all-reduce.13.cloned.1.call-update) | async-done | bytes 524304 | tf_op jit(solution)/shard_map/psum | solution.py:16
  407.9 85.2 %all-reduce.19.cloned.1.call-done = (f32[256,512]{0,1:T(8,128)}, f32[256,512]{0,1:T(8,128)}) async-done(((f32[256,512]{0,1:T(8,128)}, f32[256,512]{0,1:T(8,128)}), (f32[256,512]{0,1:T(8,128)}, f32[256,512]{0,1:T(8,128)})) %all-reduce.19.cloned.1.call-update) | async-done | bytes 1048592 | tf_op jit(solution)/shard_map/psum | solution.py:16
  496.8 11.7 cholesky.446
  508.7 9.8 custom-call.38
  521.0 11.7 cholesky.465
  534.1 10.2 custom-call.39
  545.9 11.7 cholesky.486
  558.3 9.8 custom-call.40
  569.5 11.7 cholesky.503
  584.8 8.0 while.7
  592.8 39.3 %custom-call.41 = f32[4,128,128]{1,2,0:T(8,128)S(1)} custom-call(f32[4,128,128]{2,1,0:T(8,128)S(1)} %get-tuple-element.28), custom_call_target="InvertDiagBlocksLowerTriangular" | custom-call | tf_op jit(solution)/shard_map/triangular_solve/custom-call.3 | solution.py:57
  639.6 57.4 %all-gather.7.cloned.1.call-done = bf16[4096,512]{0,1:T(8,128)(2,1)} async-done(((bf16[256,512]{0,1:T(8,128)(2,1)}), bf16[4096,512]{0,1:T(8,128)(2,1)}) %all-gather.7.cloned.1.call-update) | async-done | bytes 4194320 | tf_op jit(solution)/shard_map/all_gather | solution.py:66
  700.1 39.3 %all-gather.9.cloned.1.call-done = f32[256,4096]{0,1:T(8,128)} async-done(((f32[256,1024]{0,1:T(8,128)}), f32[256,4096]{0,1:T(8,128)}) %all-gather.9.cloned.1.call-update) | async-done | bytes 4194320 | tf_op jit(solution)/shard_map/all_gather | solution.py:100
  743.7 8.6 convolution_bitcast_fusion
  752.3 9.8 reshape.207
  762.1 11.4 copy.64
  773.5 7.0 all-to-all-start
  783.2 115.7 %all-to-all-done = f32[256,32,256]{2,0,1:T(8,128)} async-done(((f32[256,32,256]{2,0,1:T(8,128)}), f32[256,32,256]{2,0,1:T(8,128)}, u32[]{:S(2)}, u32[]{:S(2)}) %all-to-all-start) | async-done | bytes 8388640 | tf_op jit(solution)/shard_map/all_to_all | solution.py:117
  898.9 10.5 copy.92
  909.4 5.2 fusion.97
  917.8 312.3 %all-reduce.17.cloned.1.call-done = (f32[2048,256]{0,1:T(8,128)}, f32[2048,256]{0,1:T(8,128)}) async-done(((f32[2048,256]{0,1:T(8,128)}, f32[2048,256]{0,1:T(8,128)}), (f32[2048,256]{0,1:T(8,128)}, f32[2048,256]{0,1:T(8,128)})) %all-reduce.17.cloned.1.call-update) | async-done | bytes 4194320 | tf_op jit(solution)/shard_map/psum | solution.py:16
  1232.5 68.1 %all-reduce.15.cloned.1.call-done = f32[512,512]{0,1:T(8,128)} async-done(((f32[512,512]{0,1:T(8,128)}), f32[512,512]{0,1:T(8,128)}) %all-reduce.15.cloned.1.call-update) | async-done | bytes 1048592 | tf_op jit(solution)/shard_map/psum | solution.py:16
  1304.6 11.7 cholesky.518
  1316.3 9.8 custom-call.42
  1328.7 11.7 cholesky.537
  1343.3 10.6 custom-call.43
  1360.7 13.2 cholesky.558
  1378.3 11.3 custom-call.44
  1392.7 13.2 cholesky.575
  1418.0 12.0 while.5
  1430.1 40.1 %custom-call.26 = f32[4,128,128]{1,2,0:T(8,128)} custom-call(f32[4,128,128]{2,1,0:T(8,128)S(1)} %get-tuple-element.20), custom_call_target="InvertDiagBlocksLowerTriangular" | custom-call | tf_op jit(solution)/shard_map/triangular_solve | solution.py:57
  1492.7 4.5 fusion.9
  1497.1 5.8 copy.82
  1502.9 46.4 %all-gather.11.cloned.1.call-done = bf16[8192,512]{0,1:T(8,128)(2,1)} async-done(((bf16[2048,512]{0,1:T(8,128)(2,1)}), bf16[8192,512]{0,1:T(8,128)(2,1)}) %all-gather.11.cloned.1.call-update) | async-done | bytes 8388624 | tf_op jit(solution)/shard_map/all_gather | solution.py:64
  1549.3 5.0 convolution_subtract_fusion
  (237 shorter events, 149.2 us)
Async XLA Ops:
  7.2 49.8 %all-reduce.11.cloned.1.call-start = ((), (), s32[]{:S(2)}) async-start(), calls=%async_computation.1 | async-start | bytes 1048576 | tf_op jit(solution)/shard_map/psum | solution.py:16
  9.6 135.3 %all-reduce.21.cloned.1.call-start = ((), (), s32[]{:S(2)}) async-start(), calls=%async_computation.10 | async-start | bytes 2097152 | tf_op jit(solution)/shard_map/psum | solution.py:16
  59.1 300.2 %all-gather.5.cloned.1.call-start = ((), (), s32[]{:S(2)}) async-start(), calls=%async_computation.2 | async-start | bytes 4456448 | tf_op jit(solution)/shard_map/all_gather | solution.py:66
  147.8 1.0 copy-start.8
  299.3 62.6 %copy-start.9 = (f32[256,128]{0,1:T(8,128)}, f32[256,128]{0,1:T(8,128)S(1)}, u32[]{:S(2)}) copy-start(f32[256,128]{0,1:T(8,128)S(1)} %fusion.81) | copy-start | bytes 393220
  301.0 0.8 copy-start.11
  301.8 103.3 %all-reduce.13.cloned.1.call-start = ((), (), s32[]{:S(2)}) async-start(), calls=%async_computation.3 | async-start | bytes 1048576 | tf_op jit(solution)/shard_map/psum | solution.py:16
  362.0 131.0 %all-reduce.19.cloned.1.call-start = ((), (), s32[]{:S(2)}) async-start(), calls=%async_computation.9 | async-start | bytes 2097152 | tf_op jit(solution)/shard_map/psum | solution.py:16
  407.3 289.8 %all-gather.7.cloned.1.call-start = ((), (), s32[]{:S(2)}) async-start(), calls=%async_computation.4 | async-start | bytes 4456448 | tf_op jit(solution)/shard_map/all_gather | solution.py:66
  495.8 1.0 copy-start.6
  584.6 54.2 %copy-start.17 = (pred[256]{0:T(512)(128)(4,1)S(1)}, pred[256]{0:T(512)(128)(4,1)}, u32[]{:S(2)}) copy-start(pred[256]{0:T(512)(128)(4,1)} %fusion.109) | copy-start | bytes 772
  634.8 3.3 copy-start.5
  636.4 1.7 copy-start.10
  636.5 63.5 %copy-start.16 = (s32[2,24]{1,0:T(2,128)S(1)}, s32[2,24]{1,0:T(2,128)}, u32[]{:S(2)}) copy-start(s32[2,24]{1,0:T(2,128)} %param.8) | copy-start | bytes 580
  638.2 0.6 copy-start.12
  639.6 99.8 %all-gather.9.cloned.1.call-start = ((), (), s32[]{:S(2)}) async-start(), calls=%async_computation.5 | async-start | bytes 5242880 | tf_op jit(solution)/shard_map/all_gather | solution.py:100
  739.4 1.9 slice-start
  773.5 125.4 %all-to-all-start = ((f32[256,32,256]{2,0,1:T(8,128)}), f32[256,32,256]{2,0,1:T(8,128)}, u32[]{:S(2)}, u32[]{:S(2)}) async-start(f32[256,32,256]{2,0,1:T(8,128)} %copy.64), calls=%async_computation | async-start | bytes 16777216 | tf_op jit(solution)/shard_map/all_to_all | solution.py:117
  780.6 449.5 %all-reduce.17.cloned.1.call-start = ((), (), s32[]{:S(2)}) async-start(), calls=%async_computation.8 | async-start | bytes 8388608 | tf_op jit(solution)/shard_map/psum | solution.py:16
  914.6 3.2 copy-start
  917.8 382.8 %all-reduce.15.cloned.1.call-start = ((), (), s32[]{:S(2)}) async-start(), calls=%async_computation.6 | async-start | bytes 2097152 | tf_op jit(solution)/shard_map/psum | solution.py:16
  1232.4 316.9 %all-gather.11.cloned.1.call-start = ((), (), s32[]{:S(2)}) async-start(), calls=%async_computation.7 | async-start | bytes 10485760 | tf_op jit(solution)/shard_map/all_gather | solution.py:64
  1303.6 1.0 copy-start.7
  1328.7 14.6 copy-start.13
  1359.4 0.7 copy-start.14
  1470.2 4.9 copy-start.15
  1472.6 3.6 copy-start.4
  1476.2 8.0 copy-start.1
  1479.7 4.5 copy-start.2
  1484.2 1.0 copy-start.3
Sparse Core Ops, SparseCore 0:
  11.1 45.8 all-reduce.10
  60.8 84.1 all-reduce.20
  301.9 57.2 all-gather.4
  362.2 42.9 all-reduce.12
  408.9 84.1 all-reduce.18
  639.7 57.2 all-gather.6
  700.0 39.3 all-gather.8
  917.9 312.1 all-reduce.16
  1233.2 67.3 all-reduce.14
  1487.1 62.1 all-gather.10
where the time goes:
time: 1580 us; the launch traced here: 1560 us
  waiting for transfers between devices  958 us (61%)
  other arithmetic  405 us (26%)
  local copies, waits for them, and re-layouts  101 us (6%)
  matrix products  68.5 us (4%)
  between operations  23.2 us (1%)
    psum x6, waiting for transfers between devices, from_root(): return lax.psum(block, axis)  642 us
    another operation x44, other arithmetic, panel_step(): diag_factor = jnp.linalg.cholesky(diagonal)  260 us
    another operation x7, other arithmetic, panel_step(): lax.linalg.triangular_solve(diag_factor, panel_rows, left_side=False, low...  120 us
    all_to_all x1, waiting for transfers between devices, local(): lax.all_to_all(placed, ('child', 'row'), split_axis=1, concat_axis=0, til...  116 us
    all_gather x2, waiting for transfers between devices, panel_step(): all_rows = lax.all_gather(update_rows, 'row', axis=0, tiled=True)  115 us
    all_gather x1, waiting for transfers between devices, panel_step(): all_rows = lax.all_gather(update_rows, 'col', axis=0, tiled=True)  46.4 us
    all_gather x1, waiting for transfers between devices, local(): full_rows = lax.all_gather(local_tile, 'col', axis=1, tiled=True)  39.3 us
  transfers between devices with their start and end apart: 11, of which 11 were waited for; matrix products, arithmetic and copies ran while one was open for 1% of the time, Pallas kernels for 0%

commit v1 on v0

--- a/solution.py
+++ b/solution.py
@@ -97,7 +97,10 @@
     row_targets = lookup(block_maps, source_child, contrib_rows)
     row_valid = contrib_rows >= 0
     block_ids = jnp.arange(root_blocks, dtype=jnp.int32)
-    full_rows = lax.all_gather(local_tile, "col", axis=1, tiled=True)
+    peers = lax.axis_size("col")
+    blocks = jnp.stack([local_tile for _ in range(peers)])
+    blocks = lax.all_to_all(blocks, "col", split_axis=0, concat_axis=0)
+    full_rows = jnp.concatenate(blocks, axis=1)
     contrib = full_rows[:, PIV:].reshape(row_block, NCB, BLK)
     col_targets = lookup(
         block_maps, jnp.full((NCB,), child_pos, dtype=jnp.int32), jnp.arange(NCB, dtype=jnp.int32)

time: 1580 us -> 1590 us (level)
    all_to_all x0 -> x1, waiting for transfers between devices: none -> 48.6 us  [local(): blocks = lax.all_to_all(blocks, 'col', split_axis=0, concat_axis=0)]
    all_gather x1 -> x0, waiting for transfers between devices: 39.3 us -> none  [local(): full_rows = lax.all_gather(local_tile, 'col', axis=1, tiled=True)]
where the time goes in v1:
time: 1590 us; the launch traced here: 1580 us
  waiting for transfers between devices  962 us (61%)
  other arithmetic  405 us (25%)
  local copies, waits for them, and re-layouts  109 us (7%)
  matrix products  67.5 us (4%)
  between operations  22.9 us (1%)
    psum x6, waiting for transfers between devices, from_root(): return lax.psum(block, axis)  644 us
    another operation x44, other arithmetic, panel_step(): diag_factor = jnp.linalg.cholesky(diagonal)  260 us
    another operation x7, other arithmetic, panel_step(): lax.linalg.triangular_solve(diag_factor, panel_rows, left_side=False, low...  120 us
    all_gather x2, waiting for transfers between devices, panel_step(): all_rows = lax.all_gather(update_rows, 'row', axis=0, tiled=True)  115 us
    all_to_all x1, waiting for transfers between devices, local(): lax.all_to_all(placed, ('child', 'row'), split_axis=1, concat_axis=0, til...  109 us
    all_to_all x1, waiting for transfers between devices, local(): blocks = lax.all_to_all(blocks, 'col', split_axis=0, concat_axis=0)  48.6 us
    all_gather x1, waiting for transfers between devices, panel_step(): all_rows = lax.all_gather(update_rows, 'col', axis=0, tiled=True)  46.4 us
  transfers between devices with their start and end apart: 11, of which 11 were waited for; matrix products, arithmetic and copies ran while one was open for 1% of the time, Pallas kernels for 0%

profile of v1, /device:TPU:1, one launch (start us, length us, event | category | flops | bytes accessed | tf_op | source)
XLA Modules:
  0.0 1581.3 jit_solution(14065528968426397484)
XLA Ops:
  9.7 47.3 %all-reduce.11.cloned.1.call-done = f32[256,512]{0,1:T(8,128)} async-done(((f32[256,512]{0,1:T(8,128)}), f32[256,512]{0,1:T(8,128)}) %all-reduce.11.cloned.1.call-update) | async-done | bytes 524304 | tf_op jit(solution)/shard_map/psum | solution.py:16
  59.1 85.8 %all-reduce.21.cloned.1.call-done = (f32[256,512]{0,1:T(8,128)}, f32[256,512]{0,1:T(8,128)}) async-done(((f32[256,512]{0,1:T(8,128)}, f32[256,512]{0,1:T(8,128)}), (f32[256,512]{0,1:T(8,128)}, f32[256,512]{0,1:T(8,128)})) %all-reduce.21.cloned.1.call-update) | async-done | bytes 1048592 | tf_op jit(solution)/shard_map/psum | solution.py:16
  148.8 11.7 cholesky.374
  160.5 9.8 custom-call.34
  173.0 11.7 cholesky.393
  184.7 10.0 custom-call.35
  196.3 11.7 cholesky.414
  208.8 9.8 custom-call.36
  220.1 11.7 cholesky.431
  232.4 12.5 compare_reduce_fusion.10
  247.7 8.0 while.6
  255.7 39.3 %custom-call.37 = f32[4,128,128]{1,2,0:T(8,128)S(1)} custom-call(f32[4,128,128]{2,1,0:T(8,128)S(1)} %get-tuple-element.27), custom_call_target="InvertDiagBlocksLowerTriangular" | custom-call | tf_op jit(solution)/shard_map/triangular_solve/custom-call.3 | solution.py:57
  301.9 57.4 %all-gather.4.cloned.1.call-done = bf16[4096,512]{0,1:T(8,128)(2,1)} async-done(((bf16[256,512]{0,1:T(8,128)(2,1)}), bf16[4096,512]{0,1:T(8,128)(2,1)}) %all-gather.4.cloned.1.call-update) | async-done | bytes 4194320 | tf_op jit(solution)/shard_map/all_gather | solution.py:66
  362.0 43.1 %all-reduce.13.cloned.1.call-done = f32[256,512]{0,1:T(8,128)} async-done(((f32[256,512]{0,1:T(8,128)}), f32[256,512]{0,1:T(8,128)}) %all-reduce.13.cloned.1.call-update) | async-done | bytes 524304 | tf_op jit(solution)/shard_map/psum | solution.py:16
  407.9 85.2 %all-reduce.19.cloned.1.call-done = (f32[256,512]{0,1:T(8,128)}, f32[256,512]{0,1:T(8,128)}) async-done(((f32[256,512]{0,1:T(8,128)}, f32[256,512]{0,1:T(8,128)}), (f32[256,512]{0,1:T(8,128)}, f32[256,512]{0,1:T(8,128)})) %all-reduce.19.cloned.1.call-update) | async-done | bytes 1048592 | tf_op jit(solution)/shard_map/psum | solution.py:16
  496.8 11.7 cholesky.446
  508.7 9.8 custom-call.38
  521.0 11.7 cholesky.465
  534.1 10.2 custom-call.39
  545.9 11.7 cholesky.486
  558.3 9.8 custom-call.40
  569.5 11.7 cholesky.503
  584.6 8.0 while.7
  592.6 39.3 %custom-call.41 = f32[4,128,128]{1,2,0:T(8,128)S(1)} custom-call(f32[4,128,128]{2,1,0:T(8,128)S(1)} %get-tuple-element.28), custom_call_target="InvertDiagBlocksLowerTriangular" | custom-call | tf_op jit(solution)/shard_map/triangular_solve/custom-call.3 | solution.py:57
  639.4 57.4 %all-gather.6.cloned.1.call-done = bf16[4096,512]{0,1:T(8,128)(2,1)} async-done(((bf16[256,512]{0,1:T(8,128)(2,1)}), bf16[4096,512]{0,1:T(8,128)(2,1)}) %all-gather.6.cloned.1.call-update) | async-done | bytes 4194320 | tf_op jit(solution)/shard_map/all_gather | solution.py:66
  701.6 6.7 all-to-all-start
  708.5 48.6 %all-to-all-done = f32[4,256,1024]{2,1,0:T(8,128)} async-done(((f32[4,256,1024]{2,1,0:T(8,128)}), f32[4,256,1024]{2,1,0:T(8,128)}, u32[]{:S(2)}, u32[]{:S(2)}) %all-to-all-start) | async-done | bytes 4194336 | tf_op jit(solution)/shard_map/all_to_all | solution.py:102
  757.1 5.4 copy.132
  767.0 8.6 convolution_bitcast_fusion
  775.6 9.8 reshape.217
  785.4 11.4 copy.134
  796.9 6.1 all-to-all-start.1
  805.1 108.7 %all-to-all-done.1 = f32[256,32,256]{2,0,1:T(8,128)} async-done(((f32[256,32,256]{2,0,1:T(8,128)}), f32[256,32,256]{2,0,1:T(8,128)}, u32[]{:S(2)}, u32[]{:S(2)}) %all-to-all-start.1) | async-done | bytes 8388640 | tf_op jit(solution)/shard_map/all_to_all | solution.py:120
  913.8 10.5 copy.162
  924.3 5.2 fusion.97
  932.7 314.8 %all-reduce.17.cloned.1.call-done = (f32[2048,256]{0,1:T(8,128)}, f32[2048,256]{0,1:T(8,128)}) async-done(((f32[2048,256]{0,1:T(8,128)}, f32[2048,256]{0,1:T(8,128)}), (f32[2048,256]{0,1:T(8,128)}, f32[2048,256]{0,1:T(8,128)})) %all-reduce.17.cloned.1.call-update) | async-done | bytes 4194320 | tf_op jit(solution)/shard_map/psum | solution.py:16
  1250.3 67.6 %all-reduce.15.cloned.1.call-done = f32[512,512]{0,1:T(8,128)} async-done(((f32[512,512]{0,1:T(8,128)}), f32[512,512]{0,1:T(8,128)}) %all-reduce.15.cloned.1.call-update) | async-done | bytes 1048592 | tf_op jit(solution)/shard_map/psum | solution.py:16
  1321.9 11.7 cholesky.518
  1333.6 9.8 custom-call.42
  1346.0 11.7 cholesky.537
  1360.6 10.6 custom-call.43
  1377.9 13.2 cholesky.558
  1395.5 11.3 custom-call.44
  1409.9 13.2 cholesky.575
  1435.3 12.0 while.5
  1447.3 40.1 %custom-call.26 = f32[4,128,128]{1,2,0:T(8,128)} custom-call(f32[4,128,128]{2,1,0:T(8,128)S(1)} %get-tuple-element.20), custom_call_target="InvertDiagBlocksLowerTriangular" | custom-call | tf_op jit(solution)/shard_map/triangular_solve | solution.py:57
  1514.4 5.8 copy.152
  1520.2 46.4 %all-gather.8.cloned.1.call-done = bf16[8192,512]{0,1:T(8,128)(2,1)} async-done(((bf16[2048,512]{0,1:T(8,128)(2,1)}), bf16[8192,512]{0,1:T(8,128)(2,1)}) %all-gather.8.cloned.1.call-update) | async-done | bytes 8388624 | tf_op jit(solution)/shard_map/all_gather | solution.py:64
  (238 shorter events, 160.5 us)
Async XLA Ops:
  7.2 49.8 %all-reduce.11.cloned.1.call-start = ((), (), s32[]{:S(2)}) async-start(), calls=%async_computation.2 | async-start | bytes 1048576 | tf_op jit(solution)/shard_map/psum | solution.py:16
  9.6 135.3 %all-reduce.21.cloned.1.call-start = ((), (), s32[]{:S(2)}) async-start(), calls=%async_computation.10 | async-start | bytes 2097152 | tf_op jit(solution)/shard_map/psum | solution.py:16
  59.1 300.2 %all-gather.4.cloned.1.call-start = ((), (), s32[]{:S(2)}) async-start(), calls=%async_computation.3 | async-start | bytes 4456448 | tf_op jit(solution)/shard_map/all_gather | solution.py:66
  147.8 1.0 copy-start.8
  299.3 62.6 %copy-start.9 = (f32[256,128]{0,1:T(8,128)}, f32[256,128]{0,1:T(8,128)S(1)}, u32[]{:S(2)}) copy-start(f32[256,128]{0,1:T(8,128)S(1)} %fusion.81) | copy-start | bytes 393220
  301.0 0.8 copy-start.11
  301.8 103.3 %all-reduce.13.cloned.1.call-start = ((), (), s32[]{:S(2)}) async-start(), calls=%async_computation.4 | async-start | bytes 1048576 | tf_op jit(solution)/shard_map/psum | solution.py:16
  362.0 131.0 %all-reduce.19.cloned.1.call-start = ((), (), s32[]{:S(2)}) async-start(), calls=%async_computation.9 | async-start | bytes 2097152 | tf_op jit(solution)/shard_map/psum | solution.py:16
  407.3 289.6 %all-gather.6.cloned.1.call-start = ((), (), s32[]{:S(2)}) async-start(), calls=%async_computation.5 | async-start | bytes 4456448 | tf_op jit(solution)/shard_map/all_gather | solution.py:66
  495.8 1.0 copy-start.6
  584.5 54.2 %copy-start.17 = (pred[256]{0:T(512)(128)(4,1)S(1)}, pred[256]{0:T(512)(128)(4,1)}, u32[]{:S(2)}) copy-start(pred[256]{0:T(512)(128)(4,1)} %fusion.109) | copy-start | bytes 772
  634.7 3.3 copy-start.5
  636.3 1.7 copy-start.10
  638.0 0.6 copy-start.12
  701.6 6.7 copy-start.16
  701.6 55.6 %all-to-all-start = ((f32[4,256,1024]{2,1,0:T(8,128)}), f32[4,256,1024]{2,1,0:T(8,128)}, u32[]{:S(2)}, u32[]{:S(2)}) async-start(f32[4,256,1024]{2,1,0:T(8,128)} %stack.2), calls=%async_computation | async-start | bytes 8388608 | tf_op jit(solution)/shard_map/all_to_all | solution.py:102
  796.9 117.0 %all-to-all-start.1 = ((f32[256,32,256]{2,0,1:T(8,128)}), f32[256,32,256]{2,0,1:T(8,128)}, u32[]{:S(2)}, u32[]{:S(2)}) async-start(f32[256,32,256]{2,0,1:T(8,128)} %copy.134), calls=%async_computation.1 | async-start | bytes 16777216 | tf_op jit(solution)/shard_map/all_to_all | solution.py:120
  802.9 444.6 %all-reduce.17.cloned.1.call-start = ((), (), s32[]{:S(2)}) async-start(), calls=%async_computation.8 | async-start | bytes 8388608 | tf_op jit(solution)/shard_map/psum | solution.py:16
  929.5 3.2 copy-start
  932.7 385.2 %all-reduce.15.cloned.1.call-start = ((), (), s32[]{:S(2)}) async-start(), calls=%async_computation.6 | async-start | bytes 2097152 | tf_op jit(solution)/shard_map/psum | solution.py:16
  1249.8 316.8 %all-gather.8.cloned.1.call-start = ((), (), s32[]{:S(2)}) async-start(), calls=%async_computation.7 | async-start | bytes 10485760 | tf_op jit(solution)/shard_map/all_gather | solution.py:64
  1320.9 1.0 copy-start.7
  1345.9 14.6 copy-start.13
  1376.6 0.7 copy-start.14
  1487.4 4.9 copy-start.15
  1489.8 3.6 copy-start.4
  1493.4 8.0 copy-start.1
  1496.9 4.5 copy-start.2
  1501.4 1.0 copy-start.3
Sparse Core Ops, SparseCore 0:
  11.1 45.8 all-reduce.10
  60.8 84.1 all-reduce.20
  301.9 57.2 all-gather.3
  362.2 42.9 all-reduce.12
  408.9 84.1 all-reduce.18
  639.5 57.2 all-gather.5
  932.8 314.6 all-reduce.16
  1250.6 67.2 all-reduce.14
  1504.4 62.1 all-gather.7
